TPU v7x, 32 devices: a whole 2x2x4 slice. The times are simulated.
32 devices in a mesh: vocab: 8 (over y, x, core), hidden: 4 (over z).
Axes of the slice: x: 2, y: 2, z: 4, core: 2. Of those that a mesh axis runs over, the one named last changes fastest.
Arguments:
- token_ids: int32 [4096], P('vocab'), may hold values from 0 to 30719
- table: bfloat16 [30720, 128], P('vocab'), may hold values from -0.25 to 0.25
- projection: bfloat16 [128, 4096], P(None, 'hidden'), may hold values from -0.09375 to 0.09375
- grad_out: bfloat16 [4096, 4096], P('vocab', 'hidden'), may hold values from -6 to 6
Outputs:
- table_grad: float32 [30720, 128], P('vocab', 'hidden')
- projection_grad: float32 [128, 4096], P(None, 'hidden')
All inputs are finite; a program needn't handle non-finite values.
Results may differ from a plain program's by a relative error of at most 0.018.
Values may be sent and summed in bfloat16 or wider, within the bound.
A program may use at most 64 MiB of HBM per device.

v0:
```python
import jax
import jax.numpy as jnp
from jax import lax
from jax.sharding import PartitionSpec as P


def lookup_rows(token_ids, piece):
    count = piece.shape[0]
    inside = (token_ids >= 0) & (token_ids < count)
    picked = jnp.take(piece, jnp.clip(token_ids, 0, count - 1), axis=0)
    return jnp.where(inside[:, None], picked.astype(jnp.float32), 0.0)


def owner_rows(row_count, own_start, carry, pieces):
    grads_piece, ids_piece = pieces
    length = ids_piece.shape[0]
    row_ids = own_start + lax.iota(jnp.int32, row_count)

    def one_block(grads_block, ids_block):
        one_hot = (row_ids[:, None] == ids_block[None, :]).astype(jnp.bfloat16)
        return jnp.dot(one_hot, grads_block, preferred_element_type=jnp.float32)

    block = 2048
    grads_blocks = grads_piece.reshape(length // block, block, grads_piece.shape[1])
    ids_blocks = ids_piece.reshape(length // block, block)

    def scan_step(total, items):
        return (total + one_block(items[0], items[1]), None)

    total, unused = lax.scan(scan_step, carry, (grads_blocks, ids_blocks))
    return total


def on_device(token_ids, table, projection, grad_out):
    partial_grad = jnp.dot(grad_out, projection.T, preferred_element_type=jnp.float32)
    rounded = partial_grad.astype(jnp.bfloat16)
    token_grad = (
        lax.psum_scatter(rounded, "hidden", scatter_dimension=1, tiled=True)
        .astype(jnp.float32)
        .astype(jnp.bfloat16)
    )
    row_count = table.shape[0]
    looked = lookup_rows(token_ids, lax.all_gather(table, "vocab", axis=0, tiled=True))
    embedded = looked.astype(jnp.bfloat16)
    partial_proj = jnp.dot(embedded.T, grad_out, preferred_element_type=jnp.float32)
    projection_grad = lax.psum(partial_proj.astype(jnp.bfloat16), "vocab").astype(jnp.float32)
    own_start = lax.axis_index("vocab") * row_count
    empty = jnp.zeros((row_count, token_grad.shape[1]), jnp.float32)
    table_grad = owner_rows(
        row_count,
        own_start,
        empty,
        (
            lax.all_gather(token_grad, "vocab", axis=0, tiled=True),
            lax.all_gather(token_ids, "vocab", axis=0, tiled=True),
        ),
    )
    return (table_grad, projection_grad)


def solution(mesh):
    placed = (P("vocab"), P("vocab", None), P(None, "hidden"), P("vocab", "hidden"))
    return jax.shard_map(
        on_device,
        mesh=mesh,
        in_specs=placed,
        out_specs=(P("vocab", "hidden"), P(None, "hidden")),
        check_vma=False,
    )
```

profile of v0, /device:TPU:0, one launch (start us, length us, event | category | flops | bytes accessed | tf_op | source)
XLA Modules:
  0.0 138.5 jit_solution(14183271649989522370)
XLA Ops:
  8.0 0.0 copy-start
  8.0 0.0 reduce-scatter.2.cloned.1.call-start
  8.1 1.2 copy-done
  9.2 2.1 %convolution_convert_fusion.1 = bf16[512,128]{0,1:T(8,128)(2,1)} fusion(bf16[512,1024]{1,0:T(8,128)(2,1)S(1)} %copy-done, bf16[128,1024]{1,0:T(8,128)(2,1)} %param.8), kind=kOutput, calls=%fused_computation.13 | convolution fusion | flops 134283264 | bytes 1441792 | tf_op jit(solution)/shard_map/dot_general | solution.py:35
  11.3 0.0 reduce-scatter.2.cloned.1.call-update
  11.3 0.0 all-gather.3.cloned.1.call-start
  11.4 0.5 all-gather.3.cloned.1.call-update
  11.9 0.0 all-reduce.2.cloned.1.call-start
  12.0 10.5 %all-gather = s32[8,1,512]{2,1,0:T(1,128)S(1)} all-gather(s32[1,1,512]{2,1,0:T(1,128)} %bitcast.15), channel_id=1, replica_groups=mesh['vocab'=8,'hidden'=4] {'vocab'}, dimensions={0}, use_global_device_ids=true | all-gather | bytes 18432 | tf_op jit(solution)/shard_map/all_gather | solution.py:55
  22.6 0.7 compare_select_fusion
  23.3 0.7 compare_and_fusion.1
  24.0 9.8 %reduce-scatter.2.cloned.1.call-done = bf16[512,32]{0,1:T(8,128)(2,1)} async-done(((bf16[512,128]{0,1:T(8,128)(2,1)}), bf16[512,32]{0,1:T(8,128)(2,1)}) %reduce-scatter.2.cloned.1.call-update) | async-done | bytes 32784 | tf_op jit(solution)/shard_map/reduce_scatter | solution.py:38
  33.8 9.4 %all_gather.10 = bf16[4096,32]{0,1:T(8,128)(2,1)S(1)} all-gather(bf16[512,32]{0,1:T(8,128)(2,1)} %reduce-scatter.2.cloned.1.call-done), channel_id=1, replica_groups=mesh['vocab'=8,'hidden'=4] {'vocab'}, dimensions={0}, use_global_device_ids=true | all-gather | bytes 294912 | tf_op jit(solution)/shard_map/all_gather | solution.py:54
  43.3 0.5 copy.8
  43.8 25.3 %all-gather.3.cloned.1.call-done = bf16[30720,128]{1,0:T(8,128)(2,1)} async-done(((bf16[3840,128]{1,0:T(8,128)(2,1)}), bf16[30720,128]{1,0:T(8,128)(2,1)}) %all-gather.3.cloned.1.call-update) | async-done | bytes 7864336 | tf_op jit(solution)/shard_map/all_gather | solution.py:43
  69.1 5.3 %gather_fusion = bf16[512,128]{1,0:T(8,128)(2,1)S(1)} fusion(bf16[30720,128]{1,0:T(8,128)(2,1)} %all-gather.3.cloned.1.call-done, s32[1024]{0:T(1024)S(1)} %pad_clamp_fusion), kind=kCustom, calls=%fused_computation | custom fusion | bytes 264192 | tf_op jit(solution)/shard_map/jit(_take)/gather | solution.py:10
  74.4 1.3 convolution_convert_fusion
  75.7 0.0 all-reduce.2.cloned.1.call-update
  75.7 12.5 %while.11 = (s32[]{:T(128)}, f32[3840,32]{0,1:T(8,128)S(1)}, s32[2,2048]{1,0:T(2,128)S(1)}, bf16[2,2048,32]{2,1,0:T(8,128)(2,1)S(1)}, s32[]{:T(128)}, /*index=5*/s32[]{:T(128)}, s32[]{:T(128)}) while((s32[]{:T(128)}, f32[3840,32]{0,1:T(8,128)S(1)}, s32[2,2048]{1,0:T(2,128)S(1)}, bf16[2,2048,32]{2,1,0:T(8,128)(2,1)S(1)}, s32[]{:T(128)}, ...), condition=%wide.region_2.3_spmd.clone, body=%wide.region_1.2_spmd.clone.sunk | while | flops 511430400 | bytes 1563747 | solution.py:30
  75.8 6.2 %fusion.27 = f32[3840,32]{0,1:T(8,128)S(1)} fusion(s32[2048]{0:T(1024)S(1)} %bitcast.14, s32[3840]{0:T(1024)S(1)} %iota_add_fusion.2, bf16[2,2048,32]{2,1,0:T(8,128)(2,1)S(1)} %get-tuple-element.121, s32[]{:T(128)} %get-tuple-element.111, f32[3840,32]{0,1:T(8,128)S(1)} %get-tuple-element.112, pred[]{:T(512)S(6)} %compare.3), kind=kOutput, calls=%fused_computation.6.clone.1 | convolution fusion | flops 511426560 | bytes 1531909 | tf_op jit(solution)/shard_map/while/body/eval_jaxpr/dot_general | solution.py:21
  82.1 6.2 %fusion.27 = f32[3840,32]{0,1:T(8,128)S(1)} fusion(s32[2048]{0:T(1024)S(1)} %bitcast.14, s32[3840]{0:T(1024)S(1)} %iota_add_fusion.2, bf16[2,2048,32]{2,1,0:T(8,128)(2,1)S(1)} %get-tuple-element.121, s32[]{:T(128)} %get-tuple-element.111, f32[3840,32]{0,1:T(8,128)S(1)} %get-tuple-element.112, pred[]{:T(512)S(6)} %compare.3), kind=kOutput, calls=%fused_computation.6.clone.1 | convolution fusion | flops 511426560 | bytes 1531909 | tf_op jit(solution)/shard_map/while/body/eval_jaxpr/dot_general | solution.py:21
  88.3 0.0 copy-start.1
  88.3 41.0 %all-reduce.2.cloned.1.call-done = bf16[128,1024]{1,0:T(8,128)(2,1)} async-done(((bf16[128,1024]{1,0:T(8,128)(2,1)}), bf16[128,1024]{1,0:T(8,128)(2,1)}) %all-reduce.2.cloned.1.call-update) | async-done | bytes 262160 | tf_op jit(solution)/shard_map/psum | solution.py:46
  129.3 1.8 %convert_element_type.22 = f32[128,1024]{1,0:T(8,128)} convert(bf16[128,1024]{1,0:T(8,128)(2,1)} %all-reduce.2.cloned.1.call-done) | non-fusion elementwise | flops 131072 | bytes 786432 | tf_op jit(solution)/shard_map/convert_element_type | solution.py:46
  131.1 0.0 copy-done.1
  (8 shorter events, 0.1 us)
Async XLA Ops:
  8.0 1.2 copy-start
  8.0 25.8 %reduce-scatter.2.cloned.1.call-start = ((), (), s32[]{:S(2)}) async-start(), calls=%async_computation.1 | async-start | bytes 163840 | tf_op jit(solution)/shard_map/reduce_scatter | solution.py:38
  11.3 57.8 %all-gather.3.cloned.1.call-start = ((), (), s32[]{:S(2)}) async-start(), calls=%async_computation.2 | async-start | bytes 8847360 | tf_op jit(solution)/shard_map/all_gather | solution.py:43
  11.9 117.4 %all-reduce.2.cloned.1.call-start = ((), (), s32[]{:S(2)}) async-start(), calls=%async_computation.3 | async-start | bytes 524288 | tf_op jit(solution)/shard_map/psum | solution.py:46
  88.3 42.8 %copy-start.1 = (f32[3840,32]{0,1:T(8,128)}, f32[3840,32]{0,1:T(8,128)S(1)}, u32[]{:S(2)}) copy-start(f32[3840,32]{0,1:T(8,128)S(1)} %get-tuple-element.27) | copy-start | bytes 1474564
Sparse Core Ops, SparseCore 0:
  11.6 22.1 reduce-scatter.1
Sparse Core Ops, SparseCore 1:
  13.7 55.3 all-gather.2
  75.8 53.4 all-reduce.1
where the time goes:
time: 139 us
  waiting for transfers between devices  76.7 us (55%)
  blocking collectives  20 us (14%)
  matrix products  15.8 us (11%)
  between operations  15.5 us (11%)
  local copies, waits for them, and re-layouts  6.99 us (5%)
  other arithmetic  3.25 us (2%)
    psum x1, waiting for transfers between devices, on_device(): lax.psum(partial_proj.astype(jnp.bfloat16), 'vocab').astype(jnp.float32)  41 us
    all_gather x1, waiting for transfers between devices, on_device(): lax.all_gather(table, 'vocab', axis=0, tiled=True)  25.3 us
    dot_general x2, matrix products, one_block(): return jnp.dot(one_hot, grads_block, preferred_element_type=jnp.float32)  12.4 us
    all_gather x1, blocking collectives, on_device(): lax.all_gather(token_ids, 'vocab', axis=0, tiled=True)  10.5 us
    reduce_scatter x1, waiting for transfers between devices, on_device(): lax.psum_scatter(rounded, 'hidden', scatter_dimension=1, tiled=True)  9.83 us
    all_gather x1, blocking collectives, on_device(): lax.all_gather(token_grad, 'vocab', axis=0, tiled=True)  9.44 us
    gather x1, local copies, waits for them, and re-layouts, lookup_rows(): picked = jnp.take(piece, jnp.clip(token_ids, 0, count - 1), axis=0)  5.3 us
  transfers between devices with their start and end apart: 3, of which 3 were waited for; matrix products, arithmetic and copies ran while one was open for 10% of the time, Pallas kernels for 0%

commit v1 on v0

v1 whole, which is shorter than its diff:
```python
import functools

import jax
import jax.numpy as jnp
from jax import lax
from jax.experimental import pallas as pl
from jax.experimental.pallas import tpu as pltpu
from jax.sharding import PartitionSpec as P

MESH = pl.DeviceIdType.MESH
SPAN = 256
NT = (((1,), (1,)), ((), ()))


def kernel(
    nv, nh, ids_ref, table_hbm, proj_hbm, grad_hbm, rows_out, proj_out,
    table, proj, grad, ids_all, part, part_in, tg_own, tg_all, quarter_t, one_hot, spread,
    found, found_in, emb, pg, pg_in, pg_own, pg_all,
    load_sem, ids_s, ids_r, part_s, part_r, tg_s, tg_r, found_s, found_r, emb_s, emb_r, pg_s, pg_r, all_s, all_r,
):
    v = lax.axis_index("vocab")
    h = lax.axis_index("hidden")
    rows, width = table.shape
    tokens = grad.shape[0]
    cols = width // nh
    groups = pl.cdiv(rows, SPAN)
    chunk = width // nv

    loads = [
        pltpu.make_async_copy(src, dst, load_sem.at[i])
        for i, (src, dst) in enumerate(((proj_hbm, proj), (grad_hbm, grad), (table_hbm, table)))
    ]
    for load in loads:
        load.start()

    def at_v(k):
        return lax.rem(v + k, nv)

    def at_h(k):
        return lax.rem(h + k, nh)

    barrier = pltpu.get_barrier_semaphore()
    for k in range(1, nv):
        pl.semaphore_signal(barrier, inc=1, device_id={"vocab": at_v(k)}, device_id_type=MESH)
    for k in range(1, nh):
        pl.semaphore_signal(barrier, inc=1, device_id={"hidden": at_h(k)}, device_id_type=MESH)
    pl.semaphore_wait(barrier, nv + nh - 2)

    def send(src, dst, s, r, k, where):
        copy = pltpu.make_async_remote_copy(
            src_ref=src, dst_ref=dst, send_sem=s.at[k - 1], recv_sem=r.at[k - 1],
            device_id=where, device_id_type=MESH,
        )
        copy.start()
        return copy

    sent = []
    ids_c = [send(ids_ref, ids_all.at[v], ids_s, ids_r, k, {"vocab": at_v(k)}) for k in range(1, nv)]
    ids_all[v] = ids_ref[...]

    loads[0].wait()
    loads[1].wait()
    partial_t = lax.dot_general(proj[...], grad[...], NT, preferred_element_type=jnp.float32)
    for j in range(nh):
        part[j] = partial_t[j * cols:(j + 1) * cols].astype(jnp.bfloat16)
    part_c = [
        send(part.at[at_h(k)], part_in.at[h], part_s, part_r, k, {"hidden": at_h(k)}) for k in range(1, nh)
    ]

    loads[2].wait()
    pick = (
        lax.broadcasted_iota(jnp.int32, (cols, width), 1)
        == lax.broadcasted_iota(jnp.int32, (cols, width), 0) + h * cols
    ).astype(jnp.float32).astype(jnp.bfloat16)
    turned = []
    for g in range(groups):
        size = min(SPAN, rows - g * SPAN)
        piece = lax.dot_general(
            pick, table[g * SPAN:g * SPAN + size], NT, preferred_element_type=jnp.float32
        )
        if size < SPAN:
            piece = jnp.concatenate([piece, jnp.zeros((cols, SPAN - size), jnp.float32)], axis=1)
        turned.append(piece)
    quarter_t[...] = jnp.concatenate(turned, axis=0).astype(jnp.bfloat16)

    def look_up(j):
        rel = ids_all[j] - v * rows
        group = lax.shift_right_arithmetic(rel, SPAN.bit_length() - 1)
        low = jnp.bitwise_and(rel, SPAN - 1)
        hot = (lax.broadcasted_iota(jnp.int32, (SPAN, tokens), 0) == low).astype(jnp.float32).astype(jnp.bfloat16)
        one_hot[:, pl.ds(pl.multiple_of(j * tokens, tokens), tokens)] = hot
        picked = jnp.dot(quarter_t[...], hot, preferred_element_type=jnp.float32)
        total = jnp.zeros((cols, tokens), jnp.float32)
        for g in range(groups):
            total = total + jnp.where(group == g, picked[g * cols:(g + 1) * cols], 0.0)
        found[j] = total.astype(jnp.bfloat16)

    found_c = []
    for k in range(1, nv):
        ids_c[k - 1].wait_recv()
        j = at_v(nv - k)
        look_up(j)
        found_c.append(send(found.at[j], found_in.at[v], found_s, found_r, k, {"vocab": j}))
    look_up(v)

    for copy in part_c:
        copy.wait_recv()
    part_in[h] = part[h]
    token_grad = part_in[0].astype(jnp.float32)
    for j in range(1, nh):
        token_grad = token_grad + part_in[j].astype(jnp.float32)
    tg_own[...] = token_grad.astype(jnp.bfloat16)
    tg_c = [send(tg_own, tg_all.at[v], tg_s, tg_r, k, {"vocab": at_v(k)}) for k in range(1, nv)]
    tg_all[v] = tg_own[...]

    for copy in found_c:
        copy.wait_recv()
    found_in[v] = found[v]
    mine = found_in[0].astype(jnp.float32)
    for j in range(1, nv):
        mine = mine + found_in[j].astype(jnp.float32)
    emb[h] = mine.astype(jnp.bfloat16)
    emb_c = [send(emb.at[h], emb.at[h], emb_s, emb_r, k, {"hidden": at_h(k)}) for k in range(1, nh)]
    for copy in emb_c:
        copy.wait_recv()
    embedded = jnp.concatenate([emb[j].astype(jnp.float32) for j in range(nh)], axis=0).astype(jnp.bfloat16)
    partial_proj = jnp.dot(embedded, grad[...], preferred_element_type=jnp.float32)
    for j in range(nv):
        pg[j] = partial_proj[j * chunk:(j + 1) * chunk].astype(jnp.bfloat16)
    pg_c = [send(pg.at[at_v(k)], pg_in.at[v], pg_s, pg_r, k, {"vocab": at_v(k)}) for k in range(1, nv)]

    for copy in tg_c:
        copy.wait_recv()
    for j in range(nv):
        rel = ids_all[j] - v * rows
        group = lax.shift_right_arithmetic(rel, SPAN.bit_length() - 1)
        value = tg_all[j].astype(jnp.float32)
        spread[:, j * tokens:(j + 1) * tokens] = jnp.concatenate(
            [jnp.where(group == g, value, 0.0) for g in range(groups)], axis=0
        ).astype(jnp.bfloat16)
    summed = lax.dot_general(spread[...], one_hot[...], NT, preferred_element_type=jnp.float32)
    for g in range(groups):
        size = min(SPAN, rows - g * SPAN)
        rows_out[:, g * SPAN:g * SPAN + size] = summed[g * cols:(g + 1) * cols, :size]

    for copy in pg_c:
        copy.wait_recv()
    pg_in[v] = pg[v]
    total = pg_in[0].astype(jnp.float32)
    for j in range(1, nv):
        total = total + pg_in[j].astype(jnp.float32)
    pg_own[...] = total.astype(jnp.bfloat16)
    all_c = [send(pg_own, pg_all.at[v], all_s, all_r, k, {"vocab": at_v(k)}) for k in range(1, nv)]
    pg_all[v] = pg_own[...]
    for copy in all_c:
        copy.wait_recv()
    proj_out[...] = pg_all[...]
    for copy in ids_c + part_c + tg_c + found_c + emb_c + pg_c + all_c:
        copy.wait_send()


def solution(mesh):
    nv, nh = mesh.shape["vocab"], mesh.shape["hidden"]

    def on_device(token_ids, table, projection, grad_out):
        rows, width = table.shape
        tokens, hid = grad_out.shape
        cols, chunk = width // nh, width // nv
        stacked = pl.cdiv(rows, SPAN) * cols
        half = jnp.bfloat16
        vmem = pl.BlockSpec(memory_space=pltpu.VMEM)
        hbm = pl.BlockSpec(memory_space=pl.ANY)
        sems = [pltpu.SemaphoreType.DMA((3,))]
        for peers in (nv, nh, nv, nv, nh, nv, nv):
            sems += [pltpu.SemaphoreType.DMA((peers - 1,))] * 2
        rows_t, proj_grad = pl.pallas_call(
            functools.partial(kernel, nv, nh),
            out_shape=(
                jax.ShapeDtypeStruct((cols, rows), jnp.float32),
                jax.ShapeDtypeStruct((nv, chunk, hid), half),
            ),
            in_specs=[vmem, hbm, hbm, hbm],
            out_specs=(vmem, vmem),
            scratch_shapes=[
                pltpu.VMEM((rows, width), half),
                pltpu.VMEM((width, hid), half),
                pltpu.VMEM((tokens, hid), half),
                pltpu.VMEM((nv, 1, tokens), jnp.int32),
                pltpu.VMEM((nh, cols, tokens), half),
                pltpu.VMEM((nh, cols, tokens), half),
                pltpu.VMEM((cols, tokens), half),
                pltpu.VMEM((nv, cols, tokens), half),
                pltpu.VMEM((stacked, SPAN), half),
                pltpu.VMEM((SPAN, nv * tokens), half),
                pltpu.VMEM((stacked, nv * tokens), half),
                pltpu.VMEM((nv, cols, tokens), half),
                pltpu.VMEM((nv, cols, tokens), half),
                pltpu.VMEM((nh, cols, tokens), half),
                pltpu.VMEM((nv, chunk, hid), half),
                pltpu.VMEM((nv, chunk, hid), half),
                pltpu.VMEM((chunk, hid), half),
                pltpu.VMEM((nv, chunk, hid), half),
            ] + sems,
            compiler_params=pltpu.CompilerParams(collective_id=0, has_side_effects=True),
        )(token_ids.reshape(1, tokens), table, projection, grad_out)
        return rows_t.T, proj_grad.reshape(width, hid).astype(jnp.float32)

    placed = (P("vocab"), P("vocab", None), P(None, "hidden"), P("vocab", "hidden"))
    return jax.shard_map(
        on_device,
        mesh=mesh,
        in_specs=placed,
        out_specs=(P("vocab", "hidden"), P(None, "hidden")),
        check_vma=False,
    )
```

time: 139 us -> 34 us (0.24)
  waiting for transfers between devices: 76.7 us -> 0 us
  Pallas kernels: 0 us -> 30.6 us
  blocking collectives: 20 us -> 0 us
  matrix products: 15.8 us -> 0 us
  between operations: 15.5 us -> 0.65 us
  local copies, waits for them, and re-layouts: 6.99 us -> 0.78 us
  other arithmetic: 3.25 us -> 1.85 us
    psum x1 -> x0, waiting for transfers between devices: 41 us -> none  [on_device(): lax.psum(partial_proj.astype(jnp.bfloat16), 'vocab').astype(jnp.float32)]
    pallas_call x0 -> x1, Pallas kernels: none -> 30.6 us  [on_device(): pl.pallas_call(functools.partial(kernel, nv, nh), out_shape=(jax.ShapeDty...]
    all_gather x1 -> x0, waiting for transfers between devices: 25.3 us -> none  [on_device(): lax.all_gather(table, 'vocab', axis=0, tiled=True)]
    all_gather x2 -> x0, blocking collectives: 20 us -> none  [the longest x1 10.5 us: on_device(): lax.all_gather(token_ids, 'vocab', axis=0, tiled=True)]
    dot_general x4 -> x0, matrix products: 15.8 us -> none  [the longest x2 12.4 us: one_block(): return jnp.dot(one_hot, grads_block, preferred_element_type=jnp.float32)]
    reduce_scatter x1 -> x0, waiting for transfers between devices: 9.83 us -> none  [on_device(): lax.psum_scatter(rounded, 'hidden', scatter_dimension=1, tiled=True)]
    gather x1 -> x0, local copies, waits for them, and re-layouts: 5.3 us -> none  [lookup_rows(): picked = jnp.take(piece, jnp.clip(token_ids, 0, count - 1), axis=0)]
  transfers between devices with their start and end apart: 3 -> 0, of which waited for: 3 -> 0; matrix products, arithmetic and copies ran while one was open for 10% -> 0% of each run, Pallas kernels for 0% -> 0%
where the time goes in v1:
time: 34 us; the launch traced here: 33.9 us
  Pallas kernels  30.6 us (90%)
  other arithmetic  1.85 us (5%)
  local copies, waits for them, and re-layouts  0.78 us (2%)
  between operations  0.65 us (2%)
    pallas_call x1, Pallas kernels, on_device(): pl.pallas_call(functools.partial(kernel, nv, nh), out_shape=(jax.ShapeDty...  30.6 us
    convert_element_type x1, other arithmetic, on_device(): return (rows_t.T, proj_grad.reshape(width, hid).astype(jnp.float32))  1.85 us
    unnamed x3, local copies, waits for them, and re-layouts  0.78 us

profile of v1, /device:TPU:0, one launch (start us, length us, event | category | flops | bytes accessed | tf_op | source)
XLA Modules:
  0.0 33.9 jit_solution(7594878590834799262)
XLA Ops:
  0.6 30.6 %shard_map.59 = (f32[32,3840]{1,0:T(8,128)}, bf16[8,16,1024]{2,1,0:T(8,128)(2,1)}) custom-call(s32[1,512]{1,0:T(1,128)} %bitcast.6, bf16[3840,128]{1,0:T(8,128)(2,1)} %table_hbm.1, bf16[128,1024]{1,0:T(8,128)(2,1)} %proj_hbm.1, bf16[512,1024]{1,0:T(8,128)(2,1)} %grad_hbm.1), custom_call_target="tpu_custom_call" | custom-call | tf_op jit(solution)/shard_map/pallas_call | solution.py:176
  31.2 0.0 copy-start
  31.3 1.8 %bitcast_convert_fusion = f32[128,1024]{1,0:T(8,128)} fusion(bf16[8,16,1024]{2,1,0:T(8,128)(2,1)} %get-tuple-element.5), kind=kLoop, calls=%fused_computation | loop fusion | flops 131072 | bytes 786432 | tf_op jit(solution)/shard_map/convert_element_type | solution.py:206
  33.1 0.0 copy-done
  33.1 0.8 %copy.7 = f32[3840,32]{0,1:T(8,128)} copy(f32[3840,32]{0,1:T(8,128)S(1)} %bitcast.5) | data formatting | bytes 983040
Async XLA Ops:
  31.2 1.9 %copy-start = (f32[32,3840]{1,0:T(8,128)S(1)}, f32[32,3840]{1,0:T(8,128)}, u32[]{:S(2)}) copy-start(f32[32,3840]{1,0:T(8,128)} %get-tuple-element.4) | copy-start | bytes 1474564

commit v2 on v1

--- a/solution.py
+++ b/solution.py
@@ -24,7 +24,8 @@
     tokens = grad.shape[0]
     cols = width // nh
     groups = pl.cdiv(rows, SPAN)
-    chunk = width // nv
+    chunk = grad.shape[1] // nv
+    nearest = sorted(range(1, nh), key=lambda k: min(k, nh - k))
 
     loads = [
         pltpu.make_async_copy(src, dst, load_sem.at[i])
@@ -120,14 +121,40 @@
     for j in range(1, nv):
         mine = mine + found_in[j].astype(jnp.float32)
     emb[h] = mine.astype(jnp.bfloat16)
-    emb_c = [send(emb.at[h], emb.at[h], emb_s, emb_r, k, {"hidden": at_h(k)}) for k in range(1, nh)]
-    for copy in emb_c:
-        copy.wait_recv()
-    embedded = jnp.concatenate([emb[j].astype(jnp.float32) for j in range(nh)], axis=0).astype(jnp.bfloat16)
-    partial_proj = jnp.dot(embedded, grad[...], preferred_element_type=jnp.float32)
-    for j in range(nv):
-        pg[j] = partial_proj[j * chunk:(j + 1) * chunk].astype(jnp.bfloat16)
-    pg_c = [send(pg.at[at_v(k)], pg_in.at[v], pg_s, pg_r, k, {"vocab": at_v(k)}) for k in range(1, nv)]
+    emb_c = [send(emb.at[h], emb.at[h], emb_s, emb_r, k, {"hidden": at_h(k)}) for k in nearest]
+
+    piece_c, all_c = [], []
+
+    def start_piece(step, q):
+        product = jnp.dot(emb[q], grad[...], preferred_element_type=jnp.float32)
+        for j in range(nv):
+            pg[step, j] = product[:, j * chunk:(j + 1) * chunk].astype(jnp.bfloat16)
+        piece_c.append([
+            send(pg.at[step, at_v(k)], pg_in.at[step, v], pg_s.at[step], pg_r.at[step], k, {"vocab": at_v(k)})
+            for k in range(1, nv)
+        ])
+
+    def finish_piece(step, q):
+        for copy in piece_c[step]:
+            copy.wait_recv()
+        pg_in[step, v] = pg[step, v]
+        total = pg_in[step, 0].astype(jnp.float32)
+        for j in range(1, nv):
+            total = total + pg_in[step, j].astype(jnp.float32)
+        pg_own[step] = total.astype(jnp.bfloat16)
+        all_c.append([
+            send(pg_own.at[step], pg_all.at[step, v], all_s.at[step], all_r.at[step], k, {"vocab": at_v(k)})
+            for k in range(1, nv)
+        ])
+        pg_all[step, v] = pg_own[step]
+
+    quarters = [h] + [at_h(nh - k) for k in nearest]
+    start_piece(0, quarters[0])
+    for step in range(1, nh):
+        emb_c[step - 1].wait_recv()
+        start_piece(step, quarters[step])
+        finish_piece(step - 1, quarters[step - 1])
+    finish_piece(nh - 1, quarters[nh - 1])
 
     for copy in tg_c:
         copy.wait_recv()
@@ -143,19 +170,13 @@
         size = min(SPAN, rows - g * SPAN)
         rows_out[:, g * SPAN:g * SPAN + size] = summed[g * cols:(g + 1) * cols, :size]
 
-    for copy in pg_c:
-        copy.wait_recv()
-    pg_in[v] = pg[v]
-    total = pg_in[0].astype(jnp.float32)
-    for j in range(1, nv):
-        total = total + pg_in[j].astype(jnp.float32)
-    pg_own[...] = total.astype(jnp.bfloat16)
-    all_c = [send(pg_own, pg_all.at[v], all_s, all_r, k, {"vocab": at_v(k)}) for k in range(1, nv)]
-    pg_all[v] = pg_own[...]
-    for copy in all_c:
-        copy.wait_recv()
-    proj_out[...] = pg_all[...]
-    for copy in ids_c + part_c + tg_c + found_c + emb_c + pg_c + all_c:
+    for step, q in enumerate(quarters):
+        for copy in all_c[step]:
+            copy.wait_recv()
+        proj_out[pl.ds(pl.multiple_of(q * cols, cols), cols), :] = jnp.concatenate(
+            [pg_all[step, j].astype(jnp.float32) for j in range(nv)], axis=1
+        )
+    for copy in ids_c + part_c + tg_c + found_c + emb_c + sum(piece_c, []) + sum(all_c, []):
         copy.wait_send()
 
 
@@ -165,19 +186,19 @@
     def on_device(token_ids, table, projection, grad_out):
         rows, width = table.shape
         tokens, hid = grad_out.shape
-        cols, chunk = width // nh, width // nv
+        cols, chunk = width // nh, hid // nv
         stacked = pl.cdiv(rows, SPAN) * cols
         half = jnp.bfloat16
         vmem = pl.BlockSpec(memory_space=pltpu.VMEM)
         hbm = pl.BlockSpec(memory_space=pl.ANY)
         sems = [pltpu.SemaphoreType.DMA((3,))]
-        for peers in (nv, nh, nv, nv, nh, nv, nv):
-            sems += [pltpu.SemaphoreType.DMA((peers - 1,))] * 2
+        for peers in ((nv - 1,), (nh - 1,), (nv - 1,), (nv - 1,), (nh - 1,), (nh, nv - 1), (nh, nv - 1)):
+            sems += [pltpu.SemaphoreType.DMA(peers)] * 2
         rows_t, proj_grad = pl.pallas_call(
             functools.partial(kernel, nv, nh),
             out_shape=(
                 jax.ShapeDtypeStruct((cols, rows), jnp.float32),
-                jax.ShapeDtypeStruct((nv, chunk, hid), half),
+                jax.ShapeDtypeStruct((width, hid), jnp.float32),
             ),
             in_specs=[vmem, hbm, hbm, hbm],
             out_specs=(vmem, vmem),
@@ -196,14 +217,14 @@
                 pltpu.VMEM((nv, cols, tokens), half),
                 pltpu.VMEM((nv, cols, tokens), half),
                 pltpu.VMEM((nh, cols, tokens), half),
-                pltpu.VMEM((nv, chunk, hid), half),
-                pltpu.VMEM((nv, chunk, hid), half),
-                pltpu.VMEM((chunk, hid), half),
-                pltpu.VMEM((nv, chunk, hid), half),
+                pltpu.VMEM((nh, nv, cols, chunk), half),
+                pltpu.VMEM((nh, nv, cols, chunk), half),
+                pltpu.VMEM((nh, cols, chunk), half),
+                pltpu.VMEM((nh, nv, cols, chunk), half),
             ] + sems,
             compiler_params=pltpu.CompilerParams(collective_id=0, has_side_effects=True),
         )(token_ids.reshape(1, tokens), table, projection, grad_out)
-        return rows_t.T, proj_grad.reshape(width, hid).astype(jnp.float32)
+        return rows_t.T, proj_grad
 
     placed = (P("vocab"), P("vocab", None), P(None, "hidden"), P("vocab", "hidden"))
     return jax.shard_map(

time: 34 us -> 36.5 us (1.074)
  Pallas kernels: 30.6 us -> 33 us
  local copies, waits for them, and re-layouts: 0.78 us -> 2.69 us
  other arithmetic: 1.85 us -> 0 us
    pallas_call x1, Pallas kernels: 30.6 us -> 33 us  [on_device(): pl.pallas_call(functools.partial(kernel, nv, nh), out_shape=(jax.ShapeDty...]
    unnamed x3 -> x4, local copies, waits for them, and re-layouts: 0.78 us -> 2.69 us
    convert_element_type x1 -> x0, other arithmetic: 1.85 us -> none  [on_device(): return (rows_t.T, proj_grad.reshape(width, hid).astype(jnp.float32))]
where the time goes in v2:
time: 36.5 us; the launch traced here: 36.3 us
  Pallas kernels  33 us (90%)
  local copies, waits for them, and re-layouts  2.69 us (7%)
  between operations  0.65 us (2%)
    pallas_call x1, Pallas kernels, on_device(): pl.pallas_call(functools.partial(kernel, nv, nh), out_shape=(jax.ShapeDty...  33 us
    unnamed x4, local copies, waits for them, and re-layouts  2.69 us

profile of v2, /device:TPU:0, one launch (start us, length us, event | category | flops | bytes accessed | tf_op | source)
XLA Modules:
  0.0 36.3 jit_solution(10987044544082145601)
XLA Ops:
  0.6 33.0 %shard_map.59 = (f32[32,3840]{1,0:T(8,128)}, f32[128,1024]{1,0:T(8,128)}) custom-call(s32[1,512]{1,0:T(1,128)} %bitcast.3, bf16[3840,128]{1,0:T(8,128)(2,1)} %table_hbm.1, bf16[128,1024]{1,0:T(8,128)(2,1)} %proj_hbm.1, bf16[512,1024]{1,0:T(8,128)(2,1)} %grad_hbm.1), custom_call_target="tpu_custom_call" | custom-call | tf_op jit(solution)/shard_map/pallas_call | solution.py:197
  33.6 0.0 copy-start
  33.6 1.9 %copy.8 = f32[3840,32]{0,1:T(8,128)} copy(f32[3840,32]{0,1:T(8,128)} %bitcast.2) | data formatting | bytes 983040
  35.5 0.0 copy-done
  35.5 0.8 %copy.9 = f32[128,1024]{1,0:T(8,128)} copy(f32[128,1024]{1,0:T(8,128)S(1)} %copy-done) | data formatting | bytes 1048576
Async XLA Ops:
  33.6 1.9 %copy-start = (f32[128,1024]{1,0:T(8,128)S(1)}, f32[128,1024]{1,0:T(8,128)}, u32[]{:S(2)}) copy-start(f32[128,1024]{1,0:T(8,128)} %get-tuple-element.9) | copy-start | bytes 1572868

commit v3 on v1

--- a/solution.py
+++ b/solution.py
@@ -154,9 +154,21 @@
     pg_all[v] = pg_own[...]
     for copy in all_c:
         copy.wait_recv()
-    proj_out[...] = pg_all[...]
+    for j in range(nv):
+        proj_out[j * chunk:(j + 1) * chunk] = pg_all[j].astype(jnp.float32)
     for copy in ids_c + part_c + tg_c + found_c + emb_c + pg_c + all_c:
         copy.wait_send()
+
+
+def store_both(rows_in, proj_in, rows_out, proj_out, sem):
+    copies = [
+        pltpu.make_async_copy(src, dst, sem.at[i])
+        for i, (src, dst) in enumerate(((rows_in, rows_out), (proj_in, proj_out)))
+    ]
+    for copy in copies:
+        copy.start()
+    for copy in copies:
+        copy.wait()
 
 
 def solution(mesh):
@@ -176,8 +188,8 @@
         rows_t, proj_grad = pl.pallas_call(
             functools.partial(kernel, nv, nh),
             out_shape=(
-                jax.ShapeDtypeStruct((cols, rows), jnp.float32),
-                jax.ShapeDtypeStruct((nv, chunk, hid), half),
+                pltpu.VMEM((cols, rows), jnp.float32),
+                pltpu.VMEM((width, hid), jnp.float32),
             ),
             in_specs=[vmem, hbm, hbm, hbm],
             out_specs=(vmem, vmem),
@@ -203,7 +215,17 @@
             ] + sems,
             compiler_params=pltpu.CompilerParams(collective_id=0, has_side_effects=True),
         )(token_ids.reshape(1, tokens), table, projection, grad_out)
-        return rows_t.T, proj_grad.reshape(width, hid).astype(jnp.float32)
+        rows_t, proj_grad = pl.pallas_call(
+            store_both,
+            out_shape=(
+                jax.ShapeDtypeStruct((cols, rows), jnp.float32),
+                jax.ShapeDtypeStruct((width, hid), jnp.float32),
+            ),
+            in_specs=[vmem, vmem],
+            out_specs=(hbm, hbm),
+            scratch_shapes=[pltpu.SemaphoreType.DMA((2,))],
+        )(*(pltpu.with_memory_space_constraint(x, pltpu.VMEM) for x in (rows_t, proj_grad)))
+        return rows_t.T, proj_grad
 
     placed = (P("vocab"), P("vocab", None), P(None, "hidden"), P("vocab", "hidden"))
     return jax.shard_map(

time: 34 us -> 31.5 us (0.926)
  other arithmetic: 1.85 us -> 0 us
  local copies, waits for them, and re-layouts: 0.78 us -> 0 us
    convert_element_type x1 -> x0, other arithmetic: 1.85 us -> none  [on_device(): return (rows_t.T, proj_grad.reshape(width, hid).astype(jnp.float32))]
    unnamed x3 -> x0, local copies, waits for them, and re-layouts: 0.78 us -> none
    pallas_call x1 -> x2, Pallas kernels: 30.6 us -> 30.7 us  [the longest x1 29.8 us: on_device(): pl.pallas_call(functools.partial(kernel, nv, nh), out_shape=(pltpu.VMEM((...]
where the time goes in v3:
time: 31.5 us; the launch traced here: 31.4 us
  Pallas kernels  30.7 us (97%)
  between operations  0.64 us (2%)
    pallas_call x1, Pallas kernels, on_device(): pl.pallas_call(functools.partial(kernel, nv, nh), out_shape=(pltpu.VMEM((...  29.8 us
    pallas_call x1, Pallas kernels, on_device(): pl.pallas_call(store_both, out_shape=(jax.ShapeDtypeStruct((cols, rows),...  0.97 us

profile of v3, /device:TPU:0, one launch (start us, length us, event | category | flops | bytes accessed | tf_op | source)
XLA Modules:
  0.0 31.4 jit_solution(2236567476626122510)
XLA Ops:
  0.6 29.8 %shard_map.59 = (f32[32,3840]{1,0:T(8,128)S(1)}, f32[128,1024]{1,0:T(8,128)S(1)}) custom-call(s32[1,512]{1,0:T(1,128)} %bitcast.2, bf16[3840,128]{1,0:T(8,128)(2,1)} %table_hbm.1, bf16[128,1024]{1,0:T(8,128)(2,1)} %proj_hbm.1, bf16[512,1024]{1,0:T(8,128)(2,1)} %grad_hbm.1), custom_call_target="tpu_custom_call" | custom-call | tf_op jit(solution)/shard_map/pallas_call | solution.py:188
  30.4 1.0 %shard_map.60 = (f32[32,3840]{1,0:T(8,128)}, f32[128,1024]{1,0:T(8,128)}) custom-call(f32[32,3840]{1,0:T(8,128)S(1)} %get-tuple-element.6.rows_in, f32[128,1024]{1,0:T(8,128)S(1)} %get-tuple-element.7.proj_in), custom_call_target="tpu_custom_call" | custom-call | tf_op jit(solution)/shard_map/pallas_call | solution.py:218

commit v4 on v3

--- a/solution.py
+++ b/solution.py
@@ -10,6 +10,19 @@
 MESH = pl.DeviceIdType.MESH
 SPAN = 256
 NT = (((1,), (1,)), ((), ()))
+
+
+def partner(index, k):
+    bit = 1
+    while bit <= k:
+        if k & bit:
+            index = index + bit - 2 * bit * lax.rem(index // bit, 2)
+        bit *= 2
+    return index
+
+
+def far_first(n):
+    return sorted(range(1, n), key=lambda k: (-bin(k // 2).count("1"), k % 2, -k))
 
 
 def kernel(
@@ -25,6 +38,8 @@
     cols = width // nh
     groups = pl.cdiv(rows, SPAN)
     chunk = width // nv
+    v_steps = far_first(nv)
+    h_steps = sorted(range(1, nh), reverse=True)
 
     loads = [
         pltpu.make_async_copy(src, dst, load_sem.at[i])
@@ -34,10 +49,10 @@
         load.start()
 
     def at_v(k):
-        return lax.rem(v + k, nv)
+        return partner(v, k)
 
     def at_h(k):
-        return lax.rem(h + k, nh)
+        return partner(h, k)
 
     barrier = pltpu.get_barrier_semaphore()
     for k in range(1, nv):
@@ -55,7 +70,7 @@
         return copy
 
     sent = []
-    ids_c = [send(ids_ref, ids_all.at[v], ids_s, ids_r, k, {"vocab": at_v(k)}) for k in range(1, nv)]
+    ids_c = [send(ids_ref, ids_all.at[v], ids_s, ids_r, k, {"vocab": at_v(k)}) for k in v_steps]
     ids_all[v] = ids_ref[...]
 
     loads[0].wait()
@@ -64,7 +79,7 @@
     for j in range(nh):
         part[j] = partial_t[j * cols:(j + 1) * cols].astype(jnp.bfloat16)
     part_c = [
-        send(part.at[at_h(k)], part_in.at[h], part_s, part_r, k, {"hidden": at_h(k)}) for k in range(1, nh)
+        send(part.at[at_h(k)], part_in.at[h], part_s, part_r, k, {"hidden": at_h(k)}) for k in h_steps
     ]
 
     loads[2].wait()
@@ -96,9 +111,9 @@
         found[j] = total.astype(jnp.bfloat16)
 
     found_c = []
-    for k in range(1, nv):
-        ids_c[k - 1].wait_recv()
-        j = at_v(nv - k)
+    for step, k in enumerate(v_steps):
+        ids_c[step].wait_recv()
+        j = at_v(k)
         look_up(j)
         found_c.append(send(found.at[j], found_in.at[v], found_s, found_r, k, {"vocab": j}))
     look_up(v)
@@ -110,7 +125,7 @@
     for j in range(1, nh):
         token_grad = token_grad + part_in[j].astype(jnp.float32)
     tg_own[...] = token_grad.astype(jnp.bfloat16)
-    tg_c = [send(tg_own, tg_all.at[v], tg_s, tg_r, k, {"vocab": at_v(k)}) for k in range(1, nv)]
+    tg_c = [send(tg_own, tg_all.at[v], tg_s, tg_r, k, {"vocab": at_v(k)}) for k in v_steps]
     tg_all[v] = tg_own[...]
 
     for copy in found_c:
@@ -120,15 +135,33 @@
     for j in range(1, nv):
         mine = mine + found_in[j].astype(jnp.float32)
     emb[h] = mine.astype(jnp.bfloat16)
-    emb_c = [send(emb.at[h], emb.at[h], emb_s, emb_r, k, {"hidden": at_h(k)}) for k in range(1, nh)]
+    emb_c = [send(emb.at[h], emb.at[h], emb_s, emb_r, k, {"hidden": at_h(k)}) for k in h_steps]
     for copy in emb_c:
         copy.wait_recv()
     embedded = jnp.concatenate([emb[j].astype(jnp.float32) for j in range(nh)], axis=0).astype(jnp.bfloat16)
     partial_proj = jnp.dot(embedded, grad[...], preferred_element_type=jnp.float32)
-    for j in range(nv):
-        pg[j] = partial_proj[j * chunk:(j + 1) * chunk].astype(jnp.bfloat16)
-    pg_c = [send(pg.at[at_v(k)], pg_in.at[v], pg_s, pg_r, k, {"vocab": at_v(k)}) for k in range(1, nv)]
-
+    half = grad.shape[1] // 2
+    pg_c = []
+    for p in range(2):
+        for j in range(nv):
+            pg[p, j] = partial_proj[j * chunk:(j + 1) * chunk, p * half:(p + 1) * half].astype(jnp.bfloat16)
+        pg_c.append([
+            send(pg.at[p, at_v(k)], pg_in.at[p, v], pg_s.at[p], pg_r.at[p], k, {"vocab": at_v(k)}) for k in v_steps
+        ])
+
+    all_c = []
+    for p in range(2):
+        for copy in pg_c[p]:
+            copy.wait_recv()
+        pg_in[p, v] = pg[p, v]
+        total = pg_in[p, 0].astype(jnp.float32)
+        for j in range(1, nv):
+            total = total + pg_in[p, j].astype(jnp.float32)
+        pg_own[p] = total.astype(jnp.bfloat16)
+        all_c.append([
+            send(pg_own.at[p], pg_all.at[p, v], all_s.at[p], all_r.at[p], k, {"vocab": at_v(k)}) for k in v_steps
+        ])
+        pg_all[p, v] = pg_own[p]
     for copy in tg_c:
         copy.wait_recv()
     for j in range(nv):
@@ -143,20 +176,12 @@
         size = min(SPAN, rows - g * SPAN)
         rows_out[:, g * SPAN:g * SPAN + size] = summed[g * cols:(g + 1) * cols, :size]
 
-    for copy in pg_c:
-        copy.wait_recv()
-    pg_in[v] = pg[v]
-    total = pg_in[0].astype(jnp.float32)
-    for j in range(1, nv):
-        total = total + pg_in[j].astype(jnp.float32)
-    pg_own[...] = total.astype(jnp.bfloat16)
-    all_c = [send(pg_own, pg_all.at[v], all_s, all_r, k, {"vocab": at_v(k)}) for k in range(1, nv)]
-    pg_all[v] = pg_own[...]
-    for copy in all_c:
-        copy.wait_recv()
-    for j in range(nv):
-        proj_out[j * chunk:(j + 1) * chunk] = pg_all[j].astype(jnp.float32)
-    for copy in ids_c + part_c + tg_c + found_c + emb_c + pg_c + all_c:
+    for p in range(2):
+        for copy in all_c[p]:
+            copy.wait_recv()
+        for j in range(nv):
+            proj_out[j * chunk:(j + 1) * chunk, p * half:(p + 1) * half] = pg_all[p, j].astype(jnp.float32)
+    for copy in ids_c + part_c + tg_c + found_c + emb_c + sum(pg_c, []) + sum(all_c, []):
         copy.wait_send()
 
 
@@ -183,8 +208,8 @@
         vmem = pl.BlockSpec(memory_space=pltpu.VMEM)
         hbm = pl.BlockSpec(memory_space=pl.ANY)
         sems = [pltpu.SemaphoreType.DMA((3,))]
-        for peers in (nv, nh, nv, nv, nh, nv, nv):
-            sems += [pltpu.SemaphoreType.DMA((peers - 1,))] * 2
+        for peers in ((nv - 1,), (nh - 1,), (nv - 1,), (nv - 1,), (nh - 1,), (2, nv - 1), (2, nv - 1)):
+            sems += [pltpu.SemaphoreType.DMA(peers)] * 2
         rows_t, proj_grad = pl.pallas_call(
             functools.partial(kernel, nv, nh),
             out_shape=(
@@ -208,10 +233,10 @@
                 pltpu.VMEM((nv, cols, tokens), half),
                 pltpu.VMEM((nv, cols, tokens), half),
                 pltpu.VMEM((nh, cols, tokens), half),
-                pltpu.VMEM((nv, chunk, hid), half),
-                pltpu.VMEM((nv, chunk, hid), half),
-                pltpu.VMEM((chunk, hid), half),
-                pltpu.VMEM((nv, chunk, hid), half),
+                pltpu.VMEM((2, nv, chunk, hid // 2), half),
+                pltpu.VMEM((2, nv, chunk, hid // 2), half),
+                pltpu.VMEM((2, chunk, hid // 2), half),
+                pltpu.VMEM((2, nv, chunk, hid // 2), half),
             ] + sems,
             compiler_params=pltpu.CompilerParams(collective_id=0, has_side_effects=True),
         )(token_ids.reshape(1, tokens), table, projection, grad_out)

time: 31.5 us -> 31.1 us (0.987)
  Pallas kernels: 30.7 us -> 30.3 us
    pallas_call x1, Pallas kernels: 29.8 us -> 29.3 us  [on_device(): pl.pallas_call(functools.partial(kernel, nv, nh), out_shape=(pltpu.VMEM((...]
where the time goes in v4:
time: 31.1 us; the launch traced here: 30.9 us
  Pallas kernels  30.3 us (97%)
  between operations  0.64 us (2%)
    pallas_call x1, Pallas kernels, on_device(): pl.pallas_call(functools.partial(kernel, nv, nh), out_shape=(pltpu.VMEM((...  29.3 us
    pallas_call x1, Pallas kernels, on_device(): pl.pallas_call(store_both, out_shape=(jax.ShapeDtypeStruct((cols, rows),...  0.97 us

profile of v4, /device:TPU:0, one launch (start us, length us, event | category | flops | bytes accessed | tf_op | source)
XLA Modules:
  0.0 30.9 jit_solution(537268670418715687)
XLA Ops:
  0.6 29.3 %shard_map.59 = (f32[32,3840]{1,0:T(8,128)S(1)}, f32[128,1024]{1,0:T(8,128)S(1)}) custom-call(s32[1,512]{1,0:T(1,128)} %bitcast.2, bf16[3840,128]{1,0:T(8,128)(2,1)} %table_hbm.1, bf16[128,1024]{1,0:T(8,128)(2,1)} %proj_hbm.1, bf16[512,1024]{1,0:T(8,128)(2,1)} %grad_hbm.1), custom_call_target="tpu_custom_call" | custom-call | tf_op jit(solution)/shard_map/pallas_call | solution.py:213
  29.9 1.0 %shard_map.60 = (f32[32,3840]{1,0:T(8,128)}, f32[128,1024]{1,0:T(8,128)}) custom-call(f32[32,3840]{1,0:T(8,128)S(1)} %get-tuple-element.6.rows_in, f32[128,1024]{1,0:T(8,128)S(1)} %get-tuple-element.7.proj_in), custom_call_target="tpu_custom_call" | custom-call | tf_op jit(solution)/shard_map/pallas_call | solution.py:243

commit v5 on v4

--- a/solution.py
+++ b/solution.py
@@ -26,7 +26,7 @@
 
 
 def kernel(
-    nv, nh, ids_ref, table_hbm, proj_hbm, grad_hbm, rows_out, proj_out,
+    nv, nh, ids_hbm, table_hbm, proj_hbm, grad_hbm, rows_out, proj_out,
     table, proj, grad, ids_all, part, part_in, tg_own, tg_all, quarter_t, one_hot, spread,
     found, found_in, emb, pg, pg_in, pg_own, pg_all,
     load_sem, ids_s, ids_r, part_s, part_r, tg_s, tg_r, found_s, found_r, emb_s, emb_r, pg_s, pg_r, all_s, all_r,
@@ -41,13 +41,12 @@
     v_steps = far_first(nv)
     h_steps = sorted(range(1, nh), reverse=True)
 
+    ids_load = pltpu.make_async_copy(ids_hbm, ids_all.at[v], load_sem.at[3])
+    ids_load.start()
     loads = [
         pltpu.make_async_copy(src, dst, load_sem.at[i])
         for i, (src, dst) in enumerate(((proj_hbm, proj), (grad_hbm, grad), (table_hbm, table)))
     ]
-    for load in loads:
-        load.start()
-
     def at_v(k):
         return partner(v, k)
 
@@ -59,6 +58,8 @@
         pl.semaphore_signal(barrier, inc=1, device_id={"vocab": at_v(k)}, device_id_type=MESH)
     for k in range(1, nh):
         pl.semaphore_signal(barrier, inc=1, device_id={"hidden": at_h(k)}, device_id_type=MESH)
+    for load in loads:
+        load.start()
     pl.semaphore_wait(barrier, nv + nh - 2)
 
     def send(src, dst, s, r, k, where):
@@ -69,9 +70,8 @@
         copy.start()
         return copy
 
-    sent = []
-    ids_c = [send(ids_ref, ids_all.at[v], ids_s, ids_r, k, {"vocab": at_v(k)}) for k in v_steps]
-    ids_all[v] = ids_ref[...]
+    ids_load.wait()
+    ids_c = [send(ids_all.at[v], ids_all.at[v], ids_s, ids_r, k, {"vocab": at_v(k)}) for k in v_steps]
 
     loads[0].wait()
     loads[1].wait()
@@ -207,7 +207,7 @@
         half = jnp.bfloat16
         vmem = pl.BlockSpec(memory_space=pltpu.VMEM)
         hbm = pl.BlockSpec(memory_space=pl.ANY)
-        sems = [pltpu.SemaphoreType.DMA((3,))]
+        sems = [pltpu.SemaphoreType.DMA((4,))]
         for peers in ((nv - 1,), (nh - 1,), (nv - 1,), (nv - 1,), (nh - 1,), (2, nv - 1), (2, nv - 1)):
             sems += [pltpu.SemaphoreType.DMA(peers)] * 2
         rows_t, proj_grad = pl.pallas_call(
@@ -216,7 +216,7 @@
                 pltpu.VMEM((cols, rows), jnp.float32),
                 pltpu.VMEM((width, hid), jnp.float32),
             ),
-            in_specs=[vmem, hbm, hbm, hbm],
+            in_specs=[hbm, hbm, hbm, hbm],
             out_specs=(vmem, vmem),
             scratch_shapes=[
                 pltpu.VMEM((rows, width), half),

time: 31.1 us -> 30.6 us (0.984)
  Pallas kernels: 30.3 us -> 29.8 us
    pallas_call x1, Pallas kernels: 29.3 us -> 28.8 us  [on_device(): pl.pallas_call(functools.partial(kernel, nv, nh), out_shape=(pltpu.VMEM((...]
where the time goes in v5:
time: 30.6 us; the launch traced here: 30.4 us
  Pallas kernels  29.8 us (97%)
  between operations  0.64 us (2%)
    pallas_call x1, Pallas kernels, on_device(): pl.pallas_call(functools.partial(kernel, nv, nh), out_shape=(pltpu.VMEM((...  28.8 us
    pallas_call x1, Pallas kernels, on_device(): pl.pallas_call(store_both, out_shape=(jax.ShapeDtypeStruct((cols, rows),...  0.97 us

profile of v5, /device:TPU:0, one launch (start us, length us, event | category | flops | bytes accessed | tf_op | source)
XLA Modules:
  0.0 30.4 jit_solution(11153125179556643402)
XLA Ops:
  0.6 28.8 %shard_map.59 = (f32[32,3840]{1,0:T(8,128)S(1)}, f32[128,1024]{1,0:T(8,128)S(1)}) custom-call(s32[1,512]{1,0:T(1,128)} %bitcast.2, bf16[3840,128]{1,0:T(8,128)(2,1)} %table_hbm.1, bf16[128,1024]{1,0:T(8,128)(2,1)} %proj_hbm.1, bf16[512,1024]{1,0:T(8,128)(2,1)} %grad_hbm.1), custom_call_target="tpu_custom_call" | custom-call | tf_op jit(solution)/shard_map/pallas_call | solution.py:213
  29.5 1.0 %shard_map.60 = (f32[32,3840]{1,0:T(8,128)}, f32[128,1024]{1,0:T(8,128)}) custom-call(f32[32,3840]{1,0:T(8,128)S(1)} %get-tuple-element.6.rows_in, f32[128,1024]{1,0:T(8,128)S(1)} %get-tuple-element.7.proj_in), custom_call_target="tpu_custom_call" | custom-call | tf_op jit(solution)/shard_map/pallas_call | solution.py:243

commit v6 on v5

--- a/solution.py
+++ b/solution.py
@@ -118,6 +118,15 @@
         found_c.append(send(found.at[j], found_in.at[v], found_s, found_r, k, {"vocab": j}))
     look_up(v)
 
+    for copy in found_c:
+        copy.wait_recv()
+    found_in[v] = found[v]
+    mine = found_in[0].astype(jnp.float32)
+    for j in range(1, nv):
+        mine = mine + found_in[j].astype(jnp.float32)
+    emb[h] = mine.astype(jnp.bfloat16)
+    emb_c = [send(emb.at[h], emb.at[h], emb_s, emb_r, k, {"hidden": at_h(k)}) for k in h_steps]
+
     for copy in part_c:
         copy.wait_recv()
     part_in[h] = part[h]
@@ -128,14 +137,6 @@
     tg_c = [send(tg_own, tg_all.at[v], tg_s, tg_r, k, {"vocab": at_v(k)}) for k in v_steps]
     tg_all[v] = tg_own[...]
 
-    for copy in found_c:
-        copy.wait_recv()
-    found_in[v] = found[v]
-    mine = found_in[0].astype(jnp.float32)
-    for j in range(1, nv):
-        mine = mine + found_in[j].astype(jnp.float32)
-    emb[h] = mine.astype(jnp.bfloat16)
-    emb_c = [send(emb.at[h], emb.at[h], emb_s, emb_r, k, {"hidden": at_h(k)}) for k in h_steps]
     for copy in emb_c:
         copy.wait_recv()
     embedded = jnp.concatenate([emb[j].astype(jnp.float32) for j in range(nh)], axis=0).astype(jnp.bfloat16)

time: 30.6 us -> 30.2 us (0.987)
  Pallas kernels: 29.8 us -> 29.4 us
    pallas_call x1, Pallas kernels: 28.8 us -> 28.4 us  [on_device(): pl.pallas_call(functools.partial(kernel, nv, nh), out_shape=(pltpu.VMEM((...]
where the time goes in v6:
time: 30.2 us; the launch traced here: 30.1 us
  Pallas kernels  29.4 us (97%)
  between operations  0.64 us (2%)
    pallas_call x1, Pallas kernels, on_device(): pl.pallas_call(functools.partial(kernel, nv, nh), out_shape=(pltpu.VMEM((...  28.4 us
    pallas_call x1, Pallas kernels, on_device(): pl.pallas_call(store_both, out_shape=(jax.ShapeDtypeStruct((cols, rows),...  0.97 us

profile of v6, /device:TPU:0, one launch (start us, length us, event | category | flops | bytes accessed | tf_op | source)
XLA Modules:
  0.0 30.1 jit_solution(5130074155413867343)
XLA Ops:
  0.6 28.4 %shard_map.59 = (f32[32,3840]{1,0:T(8,128)S(1)}, f32[128,1024]{1,0:T(8,128)S(1)}) custom-call(s32[1,512]{1,0:T(1,128)} %bitcast.2, bf16[3840,128]{1,0:T(8,128)(2,1)} %table_hbm.1, bf16[128,1024]{1,0:T(8,128)(2,1)} %proj_hbm.1, bf16[512,1024]{1,0:T(8,128)(2,1)} %grad_hbm.1), custom_call_target="tpu_custom_call" | custom-call | tf_op jit(solution)/shard_map/pallas_call | solution.py:214
  29.1 1.0 %shard_map.60 = (f32[32,3840]{1,0:T(8,128)}, f32[128,1024]{1,0:T(8,128)}) custom-call(f32[32,3840]{1,0:T(8,128)S(1)} %get-tuple-element.6.rows_in, f32[128,1024]{1,0:T(8,128)S(1)} %get-tuple-element.7.proj_in), custom_call_target="tpu_custom_call" | custom-call | tf_op jit(solution)/shard_map/pallas_call | solution.py:244
